TPU v7x, 32 devices: a whole 2x2x4 slice. The times are simulated.
32 devices in a mesh: gx: 4 (over y, x), gy: 4 (over z), side: 2 (over core).
Axes of the slice: x: 2, y: 2, z: 4, core: 2. Of those that a mesh axis runs over, the one named last changes fastest.
Arguments:
- source: float32 [2, 4, 256, 512], P('side', None, 'gx', 'gy'), may hold values from -20 to 20
- classes: int32 [2, 4, 256, 512], P('side', None, 'gx', 'gy'), may hold values from 0 to 7
- table: float32 [2, 8, 3], replicated, may hold values from 0.1 to 10
Outputs:
- solution: float32 [2, 4, 256, 512], P('side', None, 'gx', 'gy')
- trace_change: float32 [2], replicated
All inputs are finite; a program needn't handle non-finite values.
Results may differ from a plain program's by a relative error of at most 0.0001.
Values sent between devices are 32-bit elements; how exact they have to be, the bound alone decides.
A program may use at most 64 MiB of HBM per device.

v0:
```python
import jax
import jax.numpy as jnp
from jax import lax
from jax.sharding import PartitionSpec as P

SWEEPS = 8
ITERS = 2
NCLASS = 8


relax_weight = 0.8
robin_weight = 2.0


def extended_2(cells, sides, width):
    for axis, dim in sides:
        count = lax.axis_size(axis)
        ends = count - 1
        head = lax.slice_in_dim(cells, 0, width, axis=dim)
        tail = lax.slice_in_dim(cells, cells.shape[dim] - width, cells.shape[dim], axis=dim)
        cells = jnp.concatenate(
            [
                lax.ppermute(tail, axis, [(i, (i + 1) % count) for i in range(ends)]),
                cells,
                lax.ppermute(head, axis, [((i + 1) % count, i) for i in range(ends)]),
            ],
            axis=dim,
        )
    return cells


def from_partner(block, axis, apart):
    count = lax.axis_size(axis)
    route = []
    for low in range(count):
        high = low | 1 << apart
        if high != low and high < count:
            route += [(low, high), (high, low)]
    return lax.ppermute(block, axis, route)


def lookup(classes, side_row, column):
    result = jnp.zeros(classes.shape, jnp.float32)
    for level in range(NCLASS):
        result = jnp.where(classes == level, side_row[level, column], result)
    return result


def combine(field, plane, layers, robin_data, source, cond_x, cond_y, cond_z, diagonal):
    beside = cond_x * (plane[:, 2:, 1:-1] + plane[:, :-2, 1:-1])
    beside = beside + cond_y * (plane[:, 1:-1, 2:] + plane[:, 1:-1, :-2])
    beside = beside + cond_z * (layers[2:] + layers[:-2])
    total = source + beside
    total = total.at[0].add(robin_data)
    return (1.0 - relax_weight) * field + relax_weight * total / diagonal


def on_device(source, classes, table):
    source = source[0]
    classes = classes[0]
    side_row = lax.dynamic_index_in_dim(table, lax.axis_index("side"), 0, keepdims=False)
    width_x = source.shape[1]
    width_y = source.shape[2]
    field = jnp.zeros(source.shape, jnp.float32)
    robin_data = jnp.zeros((width_x, width_y), jnp.float32)
    partials = []
    reach = SWEEPS
    stacked = jnp.stack([classes.astype(jnp.float32), source], 0)
    wide = extended_2(stacked, (("gx", 2), ("gy", 3)), reach)
    wide_classes = wide[0].astype(jnp.int32)
    wide_source = wide[1]
    wide_x = lookup(wide_classes, side_row, 0)
    wide_y = lookup(wide_classes, side_row, 1)
    wide_z = lookup(wide_classes, side_row, 2)
    start_x = lax.axis_index("gx") * width_x - reach
    start_y = lax.axis_index("gy") * width_y - reach
    rows_pos = start_x + jnp.arange(width_x + 2 * reach, dtype=jnp.int32)
    cols_pos = start_y + jnp.arange(width_y + 2 * reach, dtype=jnp.int32)
    inside_x = (rows_pos >= 0) & (rows_pos < lax.axis_size("gx") * width_x)
    inside_y = (cols_pos >= 0) & (cols_pos < lax.axis_size("gy") * width_y)
    inside = (inside_x[:, None] & inside_y[None, :])[None]
    wide_diag = 2.0 * (wide_x + wide_y + wide_z)
    wide_diag = wide_diag.at[0].add(robin_weight)
    wide_diag = jnp.where(inside, wide_diag, 1.0)
    for outer in range(ITERS):
        state = jnp.concatenate([field, robin_data[None]], 0)
        extended = extended_2(state, (("gx", 1), ("gy", 2)), reach)
        wide_field = extended[:-1]
        wide_data = extended[-1]
        for inner in range(SWEEPS):
            padded = jnp.pad(wide_field, 1)
            layers = padded[:, 1:-1, 1:-1]
            updated = combine(
                wide_field,
                padded[1:-1],
                layers,
                wide_data,
                wide_source,
                wide_x,
                wide_y,
                wide_z,
                wide_diag,
            )
            wide_field = jnp.where(inside, updated, 0.0)
        field = wide_field[:, reach : reach + width_x, reach : reach + width_y]
        outgoing = robin_weight * field[0] - robin_data
        new_data = from_partner(outgoing, "side", 0)
        partial_sum = jnp.sum((new_data - robin_data) ** 2)
        partials.append(lax.psum(partial_sum, ("gx", "gy", "side")))
        robin_data = new_data
    totals = jnp.stack(partials)
    return (field[None], jnp.sqrt(totals))


def solution(mesh):
    in_specs = (P("side", None, "gx", "gy"), P("side", None, "gx", "gy"), P())
    out_specs = (P("side", None, "gx", "gy"), P())
    return jax.shard_map(
        on_device, mesh=mesh, in_specs=in_specs, out_specs=out_specs, check_vma=False
    )
```

profile of v0, /device:TPU:0, one launch (start us, length us, event | category | flops | bytes accessed | tf_op | source)
XLA Modules:
  0.0 126.5 jit_solution(1694706204898005271)
XLA Ops:
  0.7 5.0 %collective-permute-start = (f32[5,8,128]{2,1,0:T(8,128)S(1)}, f32[5,8,128]{2,1,0:T(8,128)S(1)}, u32[]{:S(2)}, u32[]{:S(2)}) collective-permute-start(f32[5,8,128]{2,1,0:T(8,128)S(1)} %broadcast.357), channel_id=1, source_target_pairs={{0,8},{8,16},{16,24},{1,9},{9,17},{17,25},{2,10},{10,18},{18,26},{... | collective-permute-start | bytes 61448 | tf_op jit(solution)/shard_map/ppermute | solution.py:23
  5.7 1.3 %collective-permute-start.1 = (f32[5,8,128]{2,1,0:T(8,128)S(1)}, f32[5,8,128]{2,1,0:T(8,128)S(1)}, u32[]{:S(2)}, u32[]{:S(2)}) collective-permute-start(f32[5,8,128]{2,1,0:T(8,128)S(1)} %broadcast.357), channel_id=1, source_target_pairs={{8,0},{16,8},{24,16},{9,1},{17,9},{25,17},{10,2},{18,10},{26,18},{... | collective-permute-start | bytes 61448 | tf_op jit(solution)/shard_map/ppermute | solution.py:25
  7.0 0.9 convert_element_type.25
  7.9 4.5 %collective-permute-start.4 = (f32[2,4,8,128]{3,2,1,0:T(8,128)S(1)}, f32[2,4,8,128]{3,2,1,0:T(8,128)S(1)}, u32[]{:S(2)}, u32[]{:S(2)}) collective-permute-start(f32[2,4,8,128]{3,2,1,0:T(8,128)S(1)} %get-tuple-element.228), channel_id=1, source_target_pairs={{0,8},{8,16},{16,24},{1,9},{9,17},{17,25},{2,10},{10,18},{18,26},{... | collective-permute-start | bytes 98312 | tf_op jit(solution)/shard_map/ppermute | solution.py:23
  12.5 1.3 %collective-permute-start.5 = (f32[2,4,8,128]{3,2,1,0:T(8,128)S(1)}, f32[2,4,8,128]{3,2,1,0:T(8,128)S(1)}, u32[]{:S(2)}, u32[]{:S(2)}) collective-permute-start(f32[2,4,8,128]{3,2,1,0:T(8,128)S(1)} %get-tuple-element.229), channel_id=1, source_target_pairs={{8,0},{16,8},{24,16},{9,1},{17,9},{25,17},{10,2},{18,10},{26,18},{... | collective-permute-start | bytes 98312 | tf_op jit(solution)/shard_map/ppermute | solution.py:25
  13.8 0.7 fusion.176
  14.6 0.7 fusion.177
  15.4 0.1 fusion.175
  15.5 3.5 %collective-permute-start.2 = (f32[5,80,8]{2,1,0:T(8,128)S(1)}, f32[5,80,8]{2,1,0:T(8,128)S(1)}, u32[]{:S(2)}, u32[]{:S(2)}) collective-permute-start(f32[5,80,8]{2,1,0:T(8,128)S(1)} %get-tuple-element.232), channel_id=1, source_target_pairs={{0,2},{2,4},{4,6},{1,3},{3,5},{5,7},{8,10},{10,12},{12,14},{9,11},... | collective-permute-start | bytes 38408 | tf_op jit(solution)/shard_map/ppermute | solution.py:23
  19.0 1.3 %collective-permute-start.3 = (f32[5,80,8]{2,1,0:T(8,128)S(1)}, f32[5,80,8]{2,1,0:T(8,128)S(1)}, u32[]{:S(2)}, u32[]{:S(2)}) collective-permute-start(f32[5,80,8]{2,1,0:T(8,128)S(1)} %get-tuple-element.233), channel_id=1, source_target_pairs={{2,0},{4,2},{6,4},{3,1},{5,3},{7,5},{10,8},{12,10},{14,12},{11,9},... | collective-permute-start | bytes 38408 | tf_op jit(solution)/shard_map/ppermute | solution.py:25
  20.3 0.2 fusion.173
  20.5 4.6 %collective-permute-start.6 = (f32[2,4,80,8]{3,2,1,0:T(8,128)S(1)}, f32[2,4,80,8]{3,2,1,0:T(8,128)S(1)}, u32[]{:S(2)}, u32[]{:S(2)}) collective-permute-start(f32[2,4,80,8]{3,2,1,0:T(8,128)S(1)} %get-tuple-element.226), channel_id=1, source_target_pairs={{0,2},{2,4},{4,6},{1,3},{3,5},{5,7},{8,10},{10,12},{12,14},{9,11},... | collective-permute-start | bytes 61448 | tf_op jit(solution)/shard_map/ppermute | solution.py:23
  25.1 1.3 %collective-permute-start.7 = (f32[2,4,80,8]{3,2,1,0:T(8,128)S(1)}, f32[2,4,80,8]{3,2,1,0:T(8,128)S(1)}, u32[]{:S(2)}, u32[]{:S(2)}) collective-permute-start(f32[2,4,80,8]{3,2,1,0:T(8,128)S(1)} %get-tuple-element.227), channel_id=1, source_target_pairs={{2,0},{4,2},{6,4},{3,1},{5,3},{7,5},{10,8},{12,10},{14,12},{11,9},... | collective-permute-start | bytes 61448 | tf_op jit(solution)/shard_map/ppermute | solution.py:25
  26.4 0.3 collective-permute-done.3
  26.6 0.2 pad_maximum_fusion.1
  26.9 0.7 copy-done.1
  27.6 3.0 %collective-permute-done.6 = f32[2,4,80,8]{3,2,1,0:T(8,128)S(1)} collective-permute-done((f32[2,4,80,8]{3,2,1,0:T(8,128)S(1)}, f32[2,4,80,8]{3,2,1,0:T(8,128)S(1)}, u32[]{:S(2)}, u32[]{:S(2)}) %collective-permute-start.6) | collective-permute-done | bytes 20512 | tf_op jit(solution)/shard_map/ppermute | solution.py:23
  30.6 4.1 %collective-permute-done.7 = f32[2,4,80,8]{3,2,1,0:T(8,128)S(1)} collective-permute-done((f32[2,4,80,8]{3,2,1,0:T(8,128)S(1)}, f32[2,4,80,8]{3,2,1,0:T(8,128)S(1)}, u32[]{:S(2)}, u32[]{:S(2)}) %collective-permute-start.7) | collective-permute-done | bytes 20512 | tf_op jit(solution)/shard_map/ppermute | solution.py:25
  34.7 0.3 pad_maximum_fusion
  35.1 0.4 fusion.145
  35.5 15.5 %fusion.144 = (f32[4,80,144]{2,1,0:T(8,128)S(1)}, f32[1,4,80,144]{3,2,1,0:T(8,128)S(1)}, f32[1,4,80,144]{3,2,1,0:T(8,128)S(1)}, f32[1,4,80,144]{3,2,1,0:T(8,128)S(1)}) fusion(pred[1,4,80,144]{3,2,1,0:T(8,128)(4,1)S(1)} %get-tuple-element.225, pred[1,4,80,144]{3,2,1,0:T(8,128)(4,1)S(1)} %get-tuple-element.219, ...), kind=kLoop, calls=%fused_computation.247 | loop fusion | flops 1244160 | bytes 1106016 | tf_op jit(solution)/shard_map/mul | solution.py:82
  51.0 0.3 fusion.4
  51.3 0.1 fusion.169
  51.5 0.9 copy-done.2
  52.3 0.1 add_select_fusion.15
  52.4 0.3 fusion.13
  52.7 0.1 add_select_fusion.14
  52.8 0.3 fusion.22
  53.1 0.1 add_select_fusion.13
  53.2 0.3 fusion.31
  53.5 0.1 add_select_fusion.12
  53.6 0.3 fusion.40
  53.9 0.1 add_select_fusion.11
  54.0 0.3 fusion.49
  54.4 0.1 add_select_fusion.10
  54.4 0.3 fusion.58
  54.8 0.1 add_select_fusion.9
  54.9 0.3 fusion.67
  55.5 1.1 collective-permute-done.8
  56.6 1.3 %collective-permute-start.10 = (f32[5,8,128]{2,1,0:T(8,128)S(1)}, f32[5,8,128]{2,1,0:T(8,128)S(1)}, u32[]{:S(2)}, u32[]{:S(2)}) collective-permute-start(f32[5,8,128]{2,1,0:T(8,128)S(1)} %get-tuple-element.235), channel_id=1, source_target_pairs={{8,0},{16,8},{24,16},{9,1},{17,9},{25,17},{10,2},{18,10},{26,18},{... | collective-permute-start | bytes 61448 | tf_op jit(solution)/shard_map/ppermute | solution.py:25
  57.8 5.6 %collective-permute-start.9 = (f32[5,8,128]{2,1,0:T(8,128)S(1)}, f32[5,8,128]{2,1,0:T(8,128)S(1)}, u32[]{:S(2)}, u32[]{:S(2)}) collective-permute-start(f32[5,8,128]{2,1,0:T(8,128)S(1)} %get-tuple-element.234), channel_id=1, source_target_pairs={{0,8},{8,16},{16,24},{1,9},{9,17},{17,25},{2,10},{10,18},{18,26},{... | collective-permute-start | bytes 61448 | tf_op jit(solution)/shard_map/ppermute | solution.py:23
  63.4 1.5 %collective-permute-done.9 = f32[5,8,128]{2,1,0:T(8,128)S(1)} collective-permute-done((f32[5,8,128]{2,1,0:T(8,128)S(1)}, f32[5,8,128]{2,1,0:T(8,128)S(1)}, u32[]{:S(2)}, u32[]{:S(2)}) %collective-permute-start.9) | collective-permute-done | bytes 20512 | tf_op jit(solution)/shard_map/ppermute | solution.py:23
  64.9 0.1 fusion.174
  65.0 3.5 %collective-permute-start.11 = (f32[5,80,8]{2,1,0:T(8,128)S(1)}, f32[5,80,8]{2,1,0:T(8,128)S(1)}, u32[]{:S(2)}, u32[]{:S(2)}) collective-permute-start(f32[5,80,8]{2,1,0:T(8,128)S(1)} %get-tuple-element.230), channel_id=1, source_target_pairs={{0,2},{2,4},{4,6},{1,3},{3,5},{5,7},{8,10},{10,12},{12,14},{9,11},... | collective-permute-start | bytes 38408 | tf_op jit(solution)/shard_map/ppermute | solution.py:23
  68.5 1.3 %collective-permute-start.12 = (f32[5,80,8]{2,1,0:T(8,128)S(1)}, f32[5,80,8]{2,1,0:T(8,128)S(1)}, u32[]{:S(2)}, u32[]{:S(2)}) collective-permute-start(f32[5,80,8]{2,1,0:T(8,128)S(1)} %get-tuple-element.231), channel_id=1, source_target_pairs={{2,0},{4,2},{6,4},{3,1},{5,3},{7,5},{10,8},{12,10},{14,12},{11,9},... | collective-permute-start | bytes 38408 | tf_op jit(solution)/shard_map/ppermute | solution.py:25
  69.8 2.5 %collective-permute-done.11 = f32[5,80,8]{2,1,0:T(8,128)S(1)} collective-permute-done((f32[5,80,8]{2,1,0:T(8,128)S(1)}, f32[5,80,8]{2,1,0:T(8,128)S(1)}, u32[]{:S(2)}, u32[]{:S(2)}) %collective-permute-start.11) | collective-permute-done | bytes 12832 | tf_op jit(solution)/shard_map/ppermute | solution.py:23
  72.3 4.1 %collective-permute-done.12 = f32[5,80,8]{2,1,0:T(8,128)S(1)} collective-permute-done((f32[5,80,8]{2,1,0:T(8,128)S(1)}, f32[5,80,8]{2,1,0:T(8,128)S(1)}, u32[]{:S(2)}, u32[]{:S(2)}) %collective-permute-start.12) | collective-permute-done | bytes 12832 | tf_op jit(solution)/shard_map/ppermute | solution.py:25
  76.4 0.2 pad_maximum_fusion.2
  76.7 0.3 fusion.76
  76.9 0.1 fusion.160
  77.0 0.1 add_select_fusion.7
  77.1 0.3 fusion.85
  77.4 0.1 add_select_fusion.6
  77.5 0.3 fusion.94
  77.9 0.3 fusion.103
  78.4 0.3 fusion.112
  78.8 0.3 fusion.121
  79.2 0.3 fusion.130
  79.6 0.3 fusion.139
  80.1 0.8 slice_bitcast_fusion.1
  80.8 0.4 collective-permute-done.13
  81.3 0.6 multiply_reduce_fusion.1
  81.9 42.7 %all-reduce.16 = (f32[1]{0:T(128)}, f32[1]{0:T(128)}) all-reduce(f32[1]{0:T(128)} %bitcast.33, f32[1]{0:T(128)} %bitcast.31), channel_id=1, replica_groups=mesh['gx'=4,'gy'=4,'side'=2] {'gx','gy','side'}, use_global_device_ids=true, to_apply=%region_3.4 | all-reduce | flops 2 | bytes 16 | tf_op jit(solution)/shard_map/psum | solution.py:109
  124.6 1.9 %maximum_sqrt_fusion = f32[2]{0:T(128)} fusion(f32[1]{0:T(128)} %get-tuple-element.208, f32[1]{0:T(128)} %get-tuple-element.209), kind=kLoop, calls=%fused_computation.332 | loop fusion | flops 2 | bytes 16 | tf_op jit(solution)/shard_map/sqrt | solution.py:112
  (54 shorter events, 1.4 us)
Async XLA Ops:
  0.6 13.1 %copy-start = (f32[2,8,3]{1,0,2:T(2,128)S(1)}, f32[2,8,3]{1,0,2:T(2,128)}, u32[]{:S(2)}) copy-start(f32[2,8,3]{1,0,2:T(2,128)} %param.39) | copy-start | bytes 580
  0.7 7.2 %copy-start.3 = (f32[1,4,64,128]{3,2,1,0:T(8,128)S(1)}, f32[1,4,64,128]{3,2,1,0:T(8,128)}, u32[]{:S(2)}) copy-start(f32[1,4,64,128]{3,2,1,0:T(8,128)} %param.37) | copy-start | bytes 393220
  0.7 14.6 %collective-permute-start = (f32[5,8,128]{2,1,0:T(8,128)S(1)}, f32[5,8,128]{2,1,0:T(8,128)S(1)}, u32[]{:S(2)}, u32[]{:S(2)}) collective-permute-start(f32[5,8,128]{2,1,0:T(8,128)S(1)} %broadcast.357), channel_id=1, source_target_pairs={{0,8},{8,16},{16,24},{1,9},{9,17},{17,25},{2,10},{10,18},{18,26},{... | collective-permute-start | bytes 61448 | tf_op jit(solution)/shard_map/ppermute | solution.py:23
  5.7 9.7 %collective-permute-start.1 = (f32[5,8,128]{2,1,0:T(8,128)S(1)}, f32[5,8,128]{2,1,0:T(8,128)S(1)}, u32[]{:S(2)}, u32[]{:S(2)}) collective-permute-start(f32[5,8,128]{2,1,0:T(8,128)S(1)} %broadcast.357), channel_id=1, source_target_pairs={{8,0},{16,8},{24,16},{9,1},{17,9},{25,17},{10,2},{18,10},{26,18},{... | collective-permute-start | bytes 61448 | tf_op jit(solution)/shard_map/ppermute | solution.py:25
  7.9 12.4 %collective-permute-start.4 = (f32[2,4,8,128]{3,2,1,0:T(8,128)S(1)}, f32[2,4,8,128]{3,2,1,0:T(8,128)S(1)}, u32[]{:S(2)}, u32[]{:S(2)}) collective-permute-start(f32[2,4,8,128]{3,2,1,0:T(8,128)S(1)} %get-tuple-element.228), channel_id=1, source_target_pairs={{0,8},{8,16},{16,24},{1,9},{9,17},{17,25},{2,10},{10,18},{18,26},{... | collective-permute-start | bytes 98312 | tf_op jit(solution)/shard_map/ppermute | solution.py:23
  12.5 7.8 %collective-permute-start.5 = (f32[2,4,8,128]{3,2,1,0:T(8,128)S(1)}, f32[2,4,8,128]{3,2,1,0:T(8,128)S(1)}, u32[]{:S(2)}, u32[]{:S(2)}) collective-permute-start(f32[2,4,8,128]{3,2,1,0:T(8,128)S(1)} %get-tuple-element.229), channel_id=1, source_target_pairs={{8,0},{16,8},{24,16},{9,1},{17,9},{25,17},{10,2},{18,10},{26,18},{... | collective-permute-start | bytes 98312 | tf_op jit(solution)/shard_map/ppermute | solution.py:25
  15.5 10.9 %collective-permute-start.2 = (f32[5,80,8]{2,1,0:T(8,128)S(1)}, f32[5,80,8]{2,1,0:T(8,128)S(1)}, u32[]{:S(2)}, u32[]{:S(2)}) collective-permute-start(f32[5,80,8]{2,1,0:T(8,128)S(1)} %get-tuple-element.232), channel_id=1, source_target_pairs={{0,2},{2,4},{4,6},{1,3},{3,5},{5,7},{8,10},{10,12},{12,14},{9,11},... | collective-permute-start | bytes 38408 | tf_op jit(solution)/shard_map/ppermute | solution.py:23
  19.0 7.7 %collective-permute-start.3 = (f32[5,80,8]{2,1,0:T(8,128)S(1)}, f32[5,80,8]{2,1,0:T(8,128)S(1)}, u32[]{:S(2)}, u32[]{:S(2)}) collective-permute-start(f32[5,80,8]{2,1,0:T(8,128)S(1)} %get-tuple-element.233), channel_id=1, source_target_pairs={{2,0},{4,2},{6,4},{3,1},{5,3},{7,5},{10,8},{12,10},{14,12},{11,9},... | collective-permute-start | bytes 38408 | tf_op jit(solution)/shard_map/ppermute | solution.py:25
  20.5 10.1 %collective-permute-start.6 = (f32[2,4,80,8]{3,2,1,0:T(8,128)S(1)}, f32[2,4,80,8]{3,2,1,0:T(8,128)S(1)}, u32[]{:S(2)}, u32[]{:S(2)}) collective-permute-start(f32[2,4,80,8]{3,2,1,0:T(8,128)S(1)} %get-tuple-element.226), channel_id=1, source_target_pairs={{0,2},{2,4},{4,6},{1,3},{3,5},{5,7},{8,10},{10,12},{12,14},{9,11},... | collective-permute-start | bytes 61448 | tf_op jit(solution)/shard_map/ppermute | solution.py:23
  25.1 9.7 %collective-permute-start.7 = (f32[2,4,80,8]{3,2,1,0:T(8,128)S(1)}, f32[2,4,80,8]{3,2,1,0:T(8,128)S(1)}, u32[]{:S(2)}, u32[]{:S(2)}) collective-permute-start(f32[2,4,80,8]{3,2,1,0:T(8,128)S(1)} %get-tuple-element.227), channel_id=1, source_target_pairs={{2,0},{4,2},{6,4},{3,1},{5,3},{7,5},{10,8},{12,10},{14,12},{11,9},... | collective-permute-start | bytes 61448 | tf_op jit(solution)/shard_map/ppermute | solution.py:25
  26.9 0.8 copy-start.1
  35.5 15.6 %slice-start = ((f32[5,80,144]{2,1,0:T(8,128)}), f32[4,80,144]{2,1,0:T(8,128)S(1)}, s32[]{:S(2)}) async-start(f32[5,80,144]{2,1,0:T(8,128)} %copy-done.1), calls=%async_computation | async-start | bytes 655360 | tf_op jit(solution)/shard_map/slice | solution.py:88
  51.3 1.0 copy-start.2
  55.3 1.2 collective-permute-start.8
  56.6 6.9 %collective-permute-start.10 = (f32[5,8,128]{2,1,0:T(8,128)S(1)}, f32[5,8,128]{2,1,0:T(8,128)S(1)}, u32[]{:S(2)}, u32[]{:S(2)}) collective-permute-start(f32[5,8,128]{2,1,0:T(8,128)S(1)} %get-tuple-element.235), channel_id=1, source_target_pairs={{8,0},{16,8},{24,16},{9,1},{17,9},{25,17},{10,2},{18,10},{26,18},{... | collective-permute-start | bytes 61448 | tf_op jit(solution)/shard_map/ppermute | solution.py:25
  57.8 7.0 %collective-permute-start.9 = (f32[5,8,128]{2,1,0:T(8,128)S(1)}, f32[5,8,128]{2,1,0:T(8,128)S(1)}, u32[]{:S(2)}, u32[]{:S(2)}) collective-permute-start(f32[5,8,128]{2,1,0:T(8,128)S(1)} %get-tuple-element.234), channel_id=1, source_target_pairs={{0,8},{8,16},{16,24},{1,9},{9,17},{17,25},{2,10},{10,18},{18,26},{... | collective-permute-start | bytes 61448 | tf_op jit(solution)/shard_map/ppermute | solution.py:23
  65.0 7.3 %collective-permute-start.11 = (f32[5,80,8]{2,1,0:T(8,128)S(1)}, f32[5,80,8]{2,1,0:T(8,128)S(1)}, u32[]{:S(2)}, u32[]{:S(2)}) collective-permute-start(f32[5,80,8]{2,1,0:T(8,128)S(1)} %get-tuple-element.230), channel_id=1, source_target_pairs={{0,2},{2,4},{4,6},{1,3},{3,5},{5,7},{8,10},{10,12},{12,14},{9,11},... | collective-permute-start | bytes 38408 | tf_op jit(solution)/shard_map/ppermute | solution.py:23
  68.5 7.9 %collective-permute-start.12 = (f32[5,80,8]{2,1,0:T(8,128)S(1)}, f32[5,80,8]{2,1,0:T(8,128)S(1)}, u32[]{:S(2)}, u32[]{:S(2)}) collective-permute-start(f32[5,80,8]{2,1,0:T(8,128)S(1)} %get-tuple-element.231), channel_id=1, source_target_pairs={{2,0},{4,2},{6,4},{3,1},{5,3},{7,5},{10,8},{12,10},{14,12},{11,9},... | collective-permute-start | bytes 38408 | tf_op jit(solution)/shard_map/ppermute | solution.py:25
  80.0 1.2 collective-permute-start.13
where the time goes:
time: 127 us; the launch traced here: 126 us
  blocking collectives  42.7 us (34%)
  starting transfers between devices  34.4 us (27%)
  other arithmetic  26.8 us (21%)
  waiting for transfers between devices  17 us (13%)
  local copies, waits for them, and re-layouts  4.31 us (3%)
    psum x1, blocking collectives, on_device(): partials.append(lax.psum(partial_sum, ('gx', 'gy', 'side')))  42.7 us
    ppermute x6, starting transfers between devices, extended_2(): lax.ppermute(tail, axis, [(i, (i + 1) % count) for i in range(ends)])  26.6 us
    mul x1, other arithmetic, on_device(): wide_diag = 2.0 * (wide_x + wide_y + wide_z)  15.5 us
    ppermute x6, waiting for transfers between devices, extended_2(): lax.ppermute(head, axis, [((i + 1) % count, i) for i in range(ends)])  8.52 us
    ppermute x6, starting transfers between devices, extended_2(): lax.ppermute(head, axis, [((i + 1) % count, i) for i in range(ends)])  7.74 us
    ppermute x6, waiting for transfers between devices, extended_2(): lax.ppermute(tail, axis, [(i, (i + 1) % count) for i in range(ends)])  6.92 us
    add x16, other arithmetic, combine(): total = source + beside  4.44 us
  transfers between devices with their start and end apart: 14, of which 8 were waited for; matrix products, arithmetic and copies ran while one was open for 3% of the time, Pallas kernels for 0%

commit v1 on v0

v1 whole, which is shorter than its diff:
```python
import functools

import jax
import jax.numpy as jnp
from jax import lax
from jax.experimental import pallas as pl
from jax.experimental.pallas import tpu as pltpu
from jax.sharding import PartitionSpec as P

SWEEPS = 8
ITERS = 2
NCLASS = 8
REACH = SWEEPS * ITERS

relax_weight = 0.8
robin_weight = 2.0

MESH = pl.DeviceIdType.MESH
AXES = ("gx", "gy", "side")
AROUND = [(dx, dy) for dx in (-1, 0, 1) for dy in (-1, 0, 1) if (dx, dy) != (0, 0)]


def reduce_groups(sizes):
    return [("gx", "side"), ("gy",)]


def kernel(
    sizes,
    source_hbm,
    classes_hbm,
    table,
    out_hbm,
    trace,
    src,
    cls,
    pack,
    halo,
    cond,
    field,
    weight,
    mine,
    theirs,
    *rest,
):
    groups = reduce_groups(sizes)
    sums = rest[: len(groups)]
    partial, local_sem, send_sem, recv_sem, side_sem, sum_send, sum_recv, out_sem = rest[len(groups) :]
    layers, rows, lanes = source_hbm.shape[1:]
    wide = rows + 2 * REACH
    gx, gy, side = (lax.axis_index(axis) for axis in AXES)
    at = {"gx": gx, "gy": gy, "side": side}

    def exists(dx, dy):
        ok = None
        for d, axis in ((dx, "gx"), (dy, "gy")):
            if d:
                here = at[axis] > 0 if d < 0 else at[axis] < sizes[axis] - 1
                ok = here if ok is None else ok & here
        return ok

    def members(group):
        count = 1
        for axis in group:
            count *= sizes[axis]
        index = 0
        for axis in group:
            index = index * sizes[axis] + at[axis]
        for step in range(1, count):
            other = lax.rem(index + step, count)
            place = dict(at)
            left = other
            for axis in reversed(group):
                place[axis] = lax.rem(left, sizes[axis])
                left = left // sizes[axis]
            yield tuple(place[axis] for axis in AXES)

    middle = pl.ds(REACH, rows)
    load_src = pltpu.make_async_copy(source_hbm.at[0], src.at[:, middle], local_sem.at[0])
    load_cls = pltpu.make_async_copy(classes_hbm.at[0], cls.at[:, middle], local_sem.at[1])
    load_src.start()
    load_cls.start()

    barrier = pltpu.get_barrier_semaphore()
    expected = 1
    pl.semaphore_signal(barrier, inc=1, device_id=(gx, gy, 1 - side), device_id_type=MESH)
    for dx, dy in AROUND:
        ok = exists(dx, dy)
        expected = expected + ok.astype(jnp.int32)

        @pl.when(ok)
        def _():
            pl.semaphore_signal(barrier, inc=1, device_id=(gx + dx, gy + dy, side), device_id_type=MESH)

    for group in groups:
        for peer in members(group):
            pl.semaphore_signal(barrier, inc=1, device_id=peer, device_id_type=MESH)
            expected = expected + 1

    lane = lax.broadcasted_iota(jnp.int32, (8, lanes), 1)
    low = lax.broadcasted_iota(jnp.int32, (8, lanes), 0)
    scalars = [[table[side, level, column] for column in range(3)] for level in range(NCLASS)]
    columns = []
    for column in range(3):
        value = jnp.zeros((8, lanes), jnp.float32)
        for level in range(NCLASS):
            value = jnp.where(lane == level, scalars[level][column], value)
        columns.append(value)
    doubled = 2.0 * (columns[0] + columns[1] + columns[2])
    doubled = jnp.where(lane < NCLASS, doubled, 1.0)
    tables = []
    for extra in (robin_weight, 0.0):
        share = relax_weight / (doubled + extra)
        tables.append([share * column for column in columns] + [share])

    load_src.wait()
    load_cls.wait()

    lane_wide = lax.broadcasted_iota(jnp.int32, (rows, lanes), 1)
    for way, first in ((0, 0), (1, lanes - REACH)):
        packed = jnp.zeros((rows, lanes), jnp.float32)
        for strip in range(2 * layers):
            ref = src if strip < layers else cls
            value = ref[strip % layers, middle, :].astype(jnp.float32)
            shift = (strip * REACH - first) % lanes
            if shift:
                value = pltpu.roll(value, shift, 1)
            packed = jnp.where(lane_wide // REACH == strip, value, packed)
        pack[way] = packed

    pl.semaphore_wait(barrier, expected)

    copies = []

    def send(condition, source_ref, target_ref, peer):
        number = len(copies)
        copy = pltpu.make_async_remote_copy(
            src_ref=source_ref,
            dst_ref=target_ref,
            send_sem=send_sem.at[number],
            recv_sem=recv_sem.at[number],
            device_id=peer,
            device_id_type=MESH,
        )
        copies.append((condition, copy))

        @pl.when(condition)
        def _():
            copy.start()

    def strip_of(dx):
        if dx == 0:
            return middle, pl.ds(0, rows), middle
        if dx > 0:
            return pl.ds(rows, REACH), pl.ds(rows - REACH, REACH), pl.ds(0, REACH)
        return pl.ds(REACH, REACH), pl.ds(0, REACH), pl.ds(REACH + rows, REACH)

    arrive = []
    for dx, dy in sorted(AROUND, key=lambda d: -abs(d[0]) - abs(d[1])):
        held, inner, landing = strip_of(dx)
        peer = (gx + dx, gy + dy, side)
        arrive.append(exists(-dx, -dy))
        if dy == 0:
            send(exists(dx, dy), src.at[:, held], src.at[:, landing], peer)
            arrive.append(exists(-dx, -dy))
            send(exists(dx, dy), cls.at[:, held], cls.at[:, landing], peer)
        elif dy > 0:
            send(exists(dx, dy), pack.at[1, inner], halo.at[0, landing], peer)
        else:
            send(exists(dx, dy), pack.at[0, inner], halo.at[1, landing], peer)

    def lookup(kinds, wanted):
        chosen = []
        for row in wanted:
            chosen.append(jnp.take_along_axis(jnp.broadcast_to(row[:1], kinds.shape), kinds, axis=1))
        return chosen

    def settle(part, layer, span, kinds, values, ok):
        count = span.size
        wanted = lookup(kinds, tables[0 if layer == 0 else 1])
        wanted[3], values = wanted[3], wanted[3] * values
        if ok is not None:
            wanted = [jnp.where(ok, value, 0.0) for value in wanted]
            values = jnp.where(ok, values, 0.0)
        for number in range(3):
            cond[number, part, layer, span] = wanted[number]
        cond[3, part, layer, span] = values
        field[1, part, layer + 1, span] = values
        if layer == 0:
            weight[part, span] = wanted[3]

    zero = jnp.zeros((wide, lanes), jnp.float32)
    for slot in range(2):
        for part in range(2):
            field[slot, part, 0] = zero
            field[slot, part, layers + 1] = zero

    for layer in range(layers):
        settle(0, layer, middle, cls[layer, middle, :], src[layer, middle, :], None)

    for (condition, copy), here in zip(copies, arrive):

        @pl.when(here)
        def _():
            copy.wait_recv()

    for dx in (-1, 1):
        span = pl.ds(0, REACH) if dx < 0 else pl.ds(REACH + rows, REACH)
        there = exists(dx, 0)
        ok = jnp.broadcast_to(there, (REACH, lanes))
        for layer in range(layers):
            settle(0, layer, span, jnp.where(ok, cls[layer, span, :], 0), src[layer, span, :], ok)

    row = lax.broadcasted_iota(jnp.int32, (wide, lanes), 0)
    wide_lane = lax.broadcasted_iota(jnp.int32, (wide, lanes), 1)
    ok_rows = ((row >= REACH) | (gx > 0)) & ((row < REACH + rows) | (gx < sizes["gx"] - 1))
    ok_left = ok_rows & (wide_lane >= lanes - REACH) & (gy > 0)
    ok_right = ok_rows & (wide_lane < REACH) & (gy < sizes["gy"] - 1)
    ok_wide = ok_left | ok_right
    halo_left = halo[0]
    halo_right = halo[1]
    everything = pl.ds(0, wide)
    for layer in range(layers):
        found = []
        for strip in (layer, layers + layer):
            left = pltpu.roll(halo_left, (lanes - REACH - strip * REACH) % lanes, 1)
            right = pltpu.roll(halo_right, (-strip * REACH) % lanes, 1) if strip else halo_right
            found.append(jnp.where(ok_left, left, jnp.where(ok_right, right, 0.0)))
        settle(1, layer, everything, found[1].astype(jnp.int32), found[0], ok_wide)

    def relax(time, layer, first, count, parts=2):
        old, new = (time - 1) % 2, time % 2
        span = pl.ds(first, count)
        edge = lax.broadcasted_iota(jnp.int32, (count, lanes), 1)
        grow = REACH if parts == 1 else 0
        before = [field[old, part, layer + 1, span] for part in range(2)]
        from_left = [pltpu.roll(value, 1, 1) for value in before]
        from_right = [pltpu.roll(value, lanes - 1, 1) for value in before]
        for part in range(parts):
            here = before[part]
            if parts == 1:
                outer = field[old, part, layer + 1, pl.ds(first - 8, count + 16)]
                above = pltpu.roll(outer, 1, 0)[8 : 8 + count]
                below = pltpu.roll(outer, count + 15, 0)[8 : 8 + count]
            else:
                above = pltpu.roll(here, 1, 0)
                below = pltpu.roll(here, count - 1, 0)
            left = jnp.where(edge == 0, from_left[1 - part], from_left[part])
            right = jnp.where(edge == lanes - 1, from_right[1 - part], from_right[part])
            deep = field[old, part, layer, span] + field[old, part, layer + 2, span]
            value = (1.0 - relax_weight) * here + cond[3, part, layer, span]
            value = value + cond[0, part, layer, span] * (above + below)
            value = value + cond[1, part, layer, span] * (left + right)
            value = value + cond[2, part, layer, span] * deep
            field[new, part, layer + 1, span] = value

    def sweep(time, layer):
        if time <= SWEEPS:
            relax(time, layer, 0, wide)
        elif time < REACH:
            relax(time, layer, SWEEPS, wide - 2 * SWEEPS)
        else:
            relax(time, layer, REACH, rows, parts=1)

    def full(start, pairs):
        @pl.loop(0, pairs)
        def _(_):
            for time in (start, start + 1):
                for layer in range(layers):
                    sweep(time, layer)

    def head(last):
        for depth in range(layers - 1):
            time = last - (layers - 2) + depth
            for layer in range(layers - 1 - depth):
                sweep(time, layer)

    def tail(last):
        for step in range(layers - 1):
            for layer in range(layers - 1, step, -1):
                sweep(last - layer + 1 + step, layer)

    full(2, 2)
    head(SWEEPS)
    near = pl.ds(SWEEPS, wide - 2 * SWEEPS)
    for part in range(2):
        mine[part] = robin_weight * field[0, part, 1, near]
    across = pltpu.make_async_remote_copy(
        src_ref=mine,
        dst_ref=theirs,
        send_sem=side_sem.at[0],
        recv_sem=side_sem.at[1],
        device_id=(gx, gy, 1 - side),
        device_id_type=MESH,
    )
    across.start()
    tail(SWEEPS)

    for depth in range(layers - 1):
        for layer in range(1 + depth, layers):
            sweep(SWEEPS + 1 + depth, layer)
    across.wait_recv()
    for part in range(2):
        cond[3, part, 0, near] = cond[3, part, 0, near] + weight[part, near] * theirs[part]
    for depth in range(layers - 1):
        for layer in range(layers - 1 - depth):
            sweep(SWEEPS + 1 + depth + layer, layer)
    full(SWEEPS + layers, 1)
    head(REACH)

    inner = pl.ds(SWEEPS, rows)
    first_change = mine[0, inner]
    own = robin_weight * field[0, 0, 1, middle]
    second_change = own - theirs[0, inner] - first_change
    folded = []
    for change in (first_change, second_change):
        square = jnp.sum((change * change).reshape(rows // 8, 8, lanes), axis=0)
        folded.append(square + pltpu.roll(square, 4, 0))
    total = jnp.where(low < 4, folded[0], folded[1])

    def exchange(number):
        group = groups[number]
        slots = sums[number]
        peers = list(members(group))
        started = []
        for k, peer in enumerate(peers):
            copy = pltpu.make_async_remote_copy(
                src_ref=partial.at[number],
                dst_ref=slots.at[k],
                send_sem=sum_send.at[number, k],
                recv_sem=sum_recv.at[number, k],
                device_id=peer,
                device_id_type=MESH,
            )
            copy.start()
            started.append(copy)
        return started

    partial[0] = total
    started = exchange(0)
    tail(REACH)
    written = pltpu.make_async_copy(field.at[0, 0, pl.ds(1, layers), middle], out_hbm.at[0], out_sem)
    written.start()
    for number in range(len(groups)):
        for k, copy in enumerate(started):
            copy.wait_recv()
            total = total + sums[number][k]
        for copy in started:
            copy.wait_send()
        if number + 1 < len(groups):
            partial[number + 1] = total
            started = exchange(number + 1)
    for number in range(ITERS):
        part = jnp.sum(jnp.where(low // 4 == number, total, 0.0))
        root = jnp.sqrt(jnp.broadcast_to(part, (8, lanes)))
        trace[number] = root[0, 0]

    for condition, copy in copies:

        @pl.when(condition)
        def _():
            copy.wait_send()

    across.wait_send()
    written.wait()


def on_device(sizes, source, classes, table):
    layers, rows, lanes = source.shape[1:]
    wide = rows + 2 * REACH
    groups = reduce_groups(sizes)
    counts = []
    for group in groups:
        count = 1
        for axis in group:
            count *= sizes[axis]
        counts.append(count)
    near = wide - 2 * SWEEPS
    return pl.pallas_call(
        functools.partial(kernel, sizes),
        out_shape=(
            jax.ShapeDtypeStruct(source.shape, jnp.float32),
            jax.ShapeDtypeStruct((ITERS,), jnp.float32),
        ),
        in_specs=[
            pl.BlockSpec(memory_space=pl.ANY),
            pl.BlockSpec(memory_space=pl.ANY),
            pl.BlockSpec(memory_space=pltpu.SMEM),
        ],
        out_specs=(
            pl.BlockSpec(memory_space=pl.ANY),
            pl.BlockSpec(memory_space=pltpu.SMEM),
        ),
        scratch_shapes=[
            pltpu.VMEM((layers, wide, lanes), jnp.float32),
            pltpu.VMEM((layers, wide, lanes), jnp.int32),
            pltpu.VMEM((2, rows, lanes), jnp.float32),
            pltpu.VMEM((2, wide, lanes), jnp.float32),
            pltpu.VMEM((4, 2, layers, wide, lanes), jnp.float32),
            pltpu.VMEM((2, 2, layers + 2, wide, lanes), jnp.float32),
            pltpu.VMEM((2, wide, lanes), jnp.float32),
            pltpu.VMEM((2, near, lanes), jnp.float32),
            pltpu.VMEM((2, near, lanes), jnp.float32),
            *[pltpu.VMEM((count - 1, 8, lanes), jnp.float32) for count in counts],
            pltpu.VMEM((len(groups), 8, lanes), jnp.float32),
            pltpu.SemaphoreType.DMA((2,)),
            pltpu.SemaphoreType.DMA((10,)),
            pltpu.SemaphoreType.DMA((10,)),
            pltpu.SemaphoreType.DMA((2,)),
            pltpu.SemaphoreType.DMA((len(groups), max(counts))),
            pltpu.SemaphoreType.DMA((len(groups), max(counts))),
            pltpu.SemaphoreType.DMA,
        ],
        compiler_params=pltpu.CompilerParams(
            collective_id=0, has_side_effects=True, vmem_limit_bytes=48 * 2**20
        ),
    )(source, classes, table)


def solution(mesh):
    sizes = {axis: mesh.shape[axis] for axis in AXES}
    in_specs = (P("side", None, "gx", "gy"), P("side", None, "gx", "gy"), P())
    out_specs = (P("side", None, "gx", "gy"), P())
    return jax.shard_map(
        functools.partial(on_device, sizes),
        mesh=mesh,
        in_specs=in_specs,
        out_specs=out_specs,
        check_vma=False,
    )
```

time: 127 us -> 28.5 us (0.22)
  blocking collectives: 42.7 us -> 0 us
  starting transfers between devices: 34.4 us -> 0 us
  other arithmetic: 26.8 us -> 0 us
  Pallas kernels: 0 us -> 23.9 us
  waiting for transfers between devices: 17 us -> 0 us
    psum x1 -> x0, blocking collectives: 42.7 us -> none  [on_device(): partials.append(lax.psum(partial_sum, ('gx', 'gy', 'side')))]
    ppermute x14 -> x0, starting transfers between devices: 34.4 us -> none  [the longest x6 26.6 us: extended_2(): lax.ppermute(tail, axis, [(i, (i + 1) % count) for i in range(ends)])]
    pallas_call x0 -> x1, Pallas kernels: none -> 23.9 us  [on_device(): pl.pallas_call(functools.partial(kernel, sizes), out_shape=(jax.ShapeDtyp...]
    ppermute x14 -> x0, waiting for transfers between devices: 17 us -> none  [the longest x6 8.52 us: extended_2(): lax.ppermute(head, axis, [((i + 1) % count, i) for i in range(ends)])]
    mul x2 -> x0, other arithmetic: 15.6 us -> none  [the longest x1 15.5 us: on_device(): wide_diag = 2.0 * (wide_x + wide_y + wide_z)]
    add x16 -> x0, other arithmetic: 4.44 us -> none  [combine(): total = source + beside]
    unnamed x9 -> x7, local copies, waits for them, and re-layouts: 1.64 us -> 3.74 us
    slice x9 -> x0, local copies, waits for them, and re-layouts: 1.88 us -> none  [the longest x2 1.38 us: lookup(): result = jnp.where(classes == level, side_row[level, column], result)]
  transfers between devices with their start and end apart: 14 -> 0, of which waited for: 8 -> 0; matrix products, arithmetic and copies ran while one was open for 3% -> 0% of each run, Pallas kernels for 0% -> 0%
where the time goes in v1:
time: 28.5 us; the launch traced here: 28.3 us
  Pallas kernels  23.9 us (84%)
  local copies, waits for them, and re-layouts  3.74 us (13%)
  between operations  0.64 us (2%)
    pallas_call x1, Pallas kernels, on_device(): pl.pallas_call(functools.partial(kernel, sizes), out_shape=(jax.ShapeDtyp...  23.9 us
    unnamed x7, local copies, waits for them, and re-layouts  3.74 us

profile of v1, /device:TPU:0, one launch (start us, length us, event | category | flops | bytes accessed | tf_op | source)
XLA Modules:
  0.0 28.3 jit_solution(16726610732580546584)
XLA Ops:
  0.6 0.8 %copy.5.table = f32[2,8,3]{2,1,0:T(8,128)S(1)} copy(f32[2,8,3]{1,0,2:T(2,128)} %param.5) | data formatting | bytes 384 | tf_op args[2]
  1.4 0.0 copy-start
  1.4 0.9 %copy-done = f32[1,4,64,128]{3,2,1,0:T(8,128)S(1)} copy-done((f32[1,4,64,128]{3,2,1,0:T(8,128)S(1)}, f32[1,4,64,128]{3,2,1,0:T(8,128)}, u32[]{:S(2)}) %copy-start) | copy-done | bytes 131096
  2.3 0.0 copy-start.1
  2.3 0.9 %copy-done.1 = s32[1,4,64,128]{3,2,1,0:T(8,128)S(1)} copy-done((s32[1,4,64,128]{3,2,1,0:T(8,128)S(1)}, s32[1,4,64,128]{3,2,1,0:T(8,128)}, u32[]{:S(2)}) %copy-start.1) | copy-done | bytes 131096
  3.2 23.9 %shard_map.50 = (f32[1,4,64,128]{3,2,1,0:T(8,128)S(1)}, f32[2]{0:T(128)S(1)}) custom-call(f32[1,4,64,128]{3,2,1,0:T(8,128)S(1)} %copy-done, s32[1,4,64,128]{3,2,1,0:T(8,128)S(1)} %copy-done.1, f32[2,8,3]{2,1,0:T(8,128)S(1)} %copy.5.table), custom_call_target="tpu_custom_call" | custom-call | tf_op jit(solution)/shard_map/pallas_call | solution.py:378
  27.1 0.7 %copy.8 = f32[1,4,64,128]{3,2,1,0:T(8,128)} copy(f32[1,4,64,128]{3,2,1,0:T(8,128)S(1)} %get-tuple-element.4) | data formatting | bytes 262144
  27.8 0.5 %copy.9 = f32[2]{0:T(128)} copy(f32[2]{0:T(128)S(1)} %get-tuple-element.5) | data formatting | bytes 16
Async XLA Ops:
  1.4 0.9 %copy-start = (f32[1,4,64,128]{3,2,1,0:T(8,128)S(1)}, f32[1,4,64,128]{3,2,1,0:T(8,128)}, u32[]{:S(2)}) copy-start(f32[1,4,64,128]{3,2,1,0:T(8,128)} %source_hbm.1) | copy-start | bytes 393220
  2.3 0.9 %copy-start.1 = (s32[1,4,64,128]{3,2,1,0:T(8,128)S(1)}, s32[1,4,64,128]{3,2,1,0:T(8,128)}, u32[]{:S(2)}) copy-start(s32[1,4,64,128]{3,2,1,0:T(8,128)} %classes_hbm.1) | copy-start | bytes 393220

commit v2 on v1

--- a/solution.py
+++ b/solution.py
@@ -21,14 +21,14 @@
 
 
 def reduce_groups(sizes):
-    return [("gx", "side"), ("gy",)]
+    return [("gy", "side"), ("gx",)]
 
 
 def kernel(
     sizes,
     source_hbm,
     classes_hbm,
-    table,
+    table_hbm,
     out_hbm,
     trace,
     src,
@@ -44,7 +44,7 @@
 ):
     groups = reduce_groups(sizes)
     sums = rest[: len(groups)]
-    partial, local_sem, send_sem, recv_sem, side_sem, sum_send, sum_recv, out_sem = rest[len(groups) :]
+    partial, table, local_sem, send_sem, recv_sem, side_sem, sum_send, sum_recv, out_sem = rest[len(groups) :]
     layers, rows, lanes = source_hbm.shape[1:]
     wide = rows + 2 * REACH
     gx, gy, side = (lax.axis_index(axis) for axis in AXES)
@@ -74,6 +74,8 @@
                 left = left // sizes[axis]
             yield tuple(place[axis] for axis in AXES)
 
+    load_table = pltpu.make_async_copy(table_hbm, table, local_sem.at[2])
+    load_table.start()
     middle = pl.ds(REACH, rows)
     load_src = pltpu.make_async_copy(source_hbm.at[0], src.at[:, middle], local_sem.at[0])
     load_cls = pltpu.make_async_copy(classes_hbm.at[0], cls.at[:, middle], local_sem.at[1])
@@ -98,7 +100,8 @@
 
     lane = lax.broadcasted_iota(jnp.int32, (8, lanes), 1)
     low = lax.broadcasted_iota(jnp.int32, (8, lanes), 0)
-    scalars = [[table[side, level, column] for column in range(3)] for level in range(NCLASS)]
+    load_table.wait()
+    scalars = [[table[column, side, level] for column in range(3)] for level in range(NCLASS)]
     columns = []
     for column in range(3):
         value = jnp.zeros((8, lanes), jnp.float32)
@@ -340,12 +343,12 @@
     tail(REACH)
     written = pltpu.make_async_copy(field.at[0, 0, pl.ds(1, layers), middle], out_hbm.at[0], out_sem)
     written.start()
+    sent = []
     for number in range(len(groups)):
         for k, copy in enumerate(started):
             copy.wait_recv()
             total = total + sums[number][k]
-        for copy in started:
-            copy.wait_send()
+        sent += started
         if number + 1 < len(groups):
             partial[number + 1] = total
             started = exchange(number + 1)
@@ -360,6 +363,8 @@
         def _():
             copy.wait_send()
 
+    for copy in sent:
+        copy.wait_send()
     across.wait_send()
     written.wait()
 
@@ -382,9 +387,9 @@
             jax.ShapeDtypeStruct((ITERS,), jnp.float32),
         ),
         in_specs=[
-            pl.BlockSpec(memory_space=pl.ANY),
-            pl.BlockSpec(memory_space=pl.ANY),
-            pl.BlockSpec(memory_space=pltpu.SMEM),
+            pl.BlockSpec(memory_space=pltpu.HBM),
+            pl.BlockSpec(memory_space=pltpu.HBM),
+            pl.BlockSpec(memory_space=pltpu.HBM),
         ],
         out_specs=(
             pl.BlockSpec(memory_space=pl.ANY),
@@ -402,7 +407,8 @@
             pltpu.VMEM((2, near, lanes), jnp.float32),
             *[pltpu.VMEM((count - 1, 8, lanes), jnp.float32) for count in counts],
             pltpu.VMEM((len(groups), 8, lanes), jnp.float32),
-            pltpu.SemaphoreType.DMA((2,)),
+            pltpu.SMEM((3, 2, NCLASS), jnp.float32),
+            pltpu.SemaphoreType.DMA((3,)),
             pltpu.SemaphoreType.DMA((10,)),
             pltpu.SemaphoreType.DMA((10,)),
             pltpu.SemaphoreType.DMA((2,)),
@@ -411,9 +417,9 @@
             pltpu.SemaphoreType.DMA,
         ],
         compiler_params=pltpu.CompilerParams(
-            collective_id=0, has_side_effects=True, vmem_limit_bytes=48 * 2**20
+            collective_id=0, has_side_effects=True, vmem_limit_bytes=64 * 2**20
         ),
-    )(source, classes, table)
+    )(source, classes, table.transpose(2, 0, 1))
 
 
 def solution(mesh):

time: 28.5 us -> 25.7 us (0.902)
  local copies, waits for them, and re-layouts: 3.74 us -> 2.08 us
  Pallas kernels: 23.9 us -> 22.8 us
    unnamed x7 -> x4, local copies, waits for them, and re-layouts: 3.74 us -> 2.08 us
    pallas_call x1, Pallas kernels: 23.9 us -> 22.8 us  [on_device(): pl.pallas_call(functools.partial(kernel, sizes), out_shape=(jax.ShapeDtyp...]
where the time goes in v2:
time: 25.7 us; the launch traced here: 25.5 us
  Pallas kernels  22.8 us (89%)
  local copies, waits for them, and re-layouts  2.08 us (8%)
  between operations  0.65 us (3%)
    pallas_call x1, Pallas kernels, on_device(): pl.pallas_call(functools.partial(kernel, sizes), out_shape=(jax.ShapeDtyp...  22.8 us
    unnamed x4, local copies, waits for them, and re-layouts  2.08 us

profile of v2, /device:TPU:0, one launch (start us, length us, event | category | flops | bytes accessed | tf_op | source)
XLA Modules:
  0.0 25.5 jit_solution(17131553178899230971)
XLA Ops:
  0.6 22.8 %shard_map.50 = (f32[1,4,64,128]{3,2,1,0:T(8,128)}, f32[2]{0:T(128)}) custom-call(f32[1,4,64,128]{3,2,1,0:T(8,128)} %source_hbm.1, s32[1,4,64,128]{3,2,1,0:T(8,128)} %classes_hbm.1, f32[3,2,8]{2,1,0:T(2,128)} %bitcast.1), custom_call_target="tpu_custom_call" | custom-call | tf_op jit(solution)/shard_map/pallas_call | solution.py:383
  23.4 0.0 copy-start
  23.4 1.6 %copy.7 = f32[1,4,64,128]{3,2,1,0:T(8,128)} copy(f32[1,4,64,128]{3,2,1,0:T(8,128)} %get-tuple-element.4) | data formatting | bytes 262144
  25.0 0.0 copy-done
  25.0 0.5 %copy.8 = f32[2]{0:T(128)} copy(f32[2]{0:T(128)S(1)} %copy-done) | data formatting | bytes 16
Async XLA Ops:
  23.4 1.6 %copy-start = (f32[2]{0:T(128)S(1)}, f32[2]{0:T(128)}, u32[]{:S(2)}) copy-start(f32[2]{0:T(128)} %get-tuple-element.5) | copy-start | bytes 28

commit v3 on v2

--- a/solution.py
+++ b/solution.py
@@ -21,7 +21,9 @@
 
 
 def reduce_groups(sizes):
-    return [("gy", "side"), ("gx",)]
+    if sizes["gx"] * sizes["gy"] * sizes["side"] <= 64:
+        return [("gx", "gy", "side")]
+    return [("gx", "side"), ("gy",)]
 
 
 def kernel(
@@ -30,7 +32,7 @@
     classes_hbm,
     table_hbm,
     out_hbm,
-    trace,
+    totals,
     src,
     cls,
     pack,
@@ -59,20 +61,15 @@
         return ok
 
     def members(group):
-        count = 1
+        places = [{}]
         for axis in group:
-            count *= sizes[axis]
-        index = 0
-        for axis in group:
-            index = index * sizes[axis] + at[axis]
-        for step in range(1, count):
-            other = lax.rem(index + step, count)
-            place = dict(at)
-            left = other
-            for axis in reversed(group):
-                place[axis] = lax.rem(left, sizes[axis])
-                left = left // sizes[axis]
-            yield tuple(place[axis] for axis in AXES)
+            turned = [at[axis]]
+            for step in range(1, sizes[axis]):
+                turned.append(jnp.where(at[axis] >= sizes[axis] - step, at[axis] + (step - sizes[axis]), at[axis] + step))
+            places = [{**place, axis: here} for place in places for here in turned]
+        return [tuple({**at, **place}[axis] for axis in AXES) for place in places[1:]]
+
+    peers_of = [members(group) for group in groups]
 
     load_table = pltpu.make_async_copy(table_hbm, table, local_sem.at[2])
     load_table.start()
@@ -93,13 +90,12 @@
         def _():
             pl.semaphore_signal(barrier, inc=1, device_id=(gx + dx, gy + dy, side), device_id_type=MESH)
 
-    for group in groups:
-        for peer in members(group):
+    for peers in peers_of:
+        for peer in peers:
             pl.semaphore_signal(barrier, inc=1, device_id=peer, device_id_type=MESH)
             expected = expected + 1
 
     lane = lax.broadcasted_iota(jnp.int32, (8, lanes), 1)
-    low = lax.broadcasted_iota(jnp.int32, (8, lanes), 0)
     load_table.wait()
     scalars = [[table[column, side, level] for column in range(3)] for level in range(NCLASS)]
     columns = []
@@ -316,14 +312,13 @@
     second_change = own - theirs[0, inner] - first_change
     folded = []
     for change in (first_change, second_change):
-        square = jnp.sum((change * change).reshape(rows // 8, 8, lanes), axis=0)
-        folded.append(square + pltpu.roll(square, 4, 0))
-    total = jnp.where(low < 4, folded[0], folded[1])
+        square = jnp.sum(change * change, axis=0, keepdims=True)
+        folded.append(square + pltpu.roll(square, lanes // 2, 1))
+    total = jnp.where(lane[:1] < lanes // 2, folded[0], folded[1])
 
     def exchange(number):
-        group = groups[number]
         slots = sums[number]
-        peers = list(members(group))
+        peers = peers_of[number]
         started = []
         for k, peer in enumerate(peers):
             copy = pltpu.make_async_remote_copy(
@@ -352,11 +347,7 @@
         if number + 1 < len(groups):
             partial[number + 1] = total
             started = exchange(number + 1)
-    for number in range(ITERS):
-        part = jnp.sum(jnp.where(low // 4 == number, total, 0.0))
-        root = jnp.sqrt(jnp.broadcast_to(part, (8, lanes)))
-        trace[number] = root[0, 0]
-
+    totals[...] = total
     for condition, copy in copies:
 
         @pl.when(condition)
@@ -367,6 +358,19 @@
         copy.wait_send()
     across.wait_send()
     written.wait()
+
+
+def finish(held, totals, out_hbm, trace, sem):
+    copy = pltpu.make_async_copy(held, out_hbm, sem)
+    copy.start()
+    total = totals[...]
+    half = total.shape[1] // 2
+    lane = lax.broadcasted_iota(jnp.int32, total.shape, 1)
+    for number in range(ITERS):
+        part = jnp.sum(jnp.where(lane // half == number, total, 0.0))
+        root = jnp.sqrt(jnp.broadcast_to(part, total.shape))
+        trace[number] = root[0, 0]
+    copy.wait()
 
 
 def on_device(sizes, source, classes, table):
@@ -380,11 +384,11 @@
             count *= sizes[axis]
         counts.append(count)
     near = wide - 2 * SWEEPS
-    return pl.pallas_call(
+    held, totals = pl.pallas_call(
         functools.partial(kernel, sizes),
         out_shape=(
-            jax.ShapeDtypeStruct(source.shape, jnp.float32),
-            jax.ShapeDtypeStruct((ITERS,), jnp.float32),
+            pltpu.VMEM(source.shape, jnp.float32),
+            pltpu.VMEM((1, lanes), jnp.float32),
         ),
         in_specs=[
             pl.BlockSpec(memory_space=pltpu.HBM),
@@ -393,7 +397,7 @@
         ],
         out_specs=(
             pl.BlockSpec(memory_space=pl.ANY),
-            pl.BlockSpec(memory_space=pltpu.SMEM),
+            pl.BlockSpec(memory_space=pltpu.VMEM),
         ),
         scratch_shapes=[
             pltpu.VMEM((layers, wide, lanes), jnp.float32),
@@ -405,8 +409,8 @@
             pltpu.VMEM((2, wide, lanes), jnp.float32),
             pltpu.VMEM((2, near, lanes), jnp.float32),
             pltpu.VMEM((2, near, lanes), jnp.float32),
-            *[pltpu.VMEM((count - 1, 8, lanes), jnp.float32) for count in counts],
-            pltpu.VMEM((len(groups), 8, lanes), jnp.float32),
+            *[pltpu.VMEM((count - 1, 1, lanes), jnp.float32) for count in counts],
+            pltpu.VMEM((len(groups), 1, lanes), jnp.float32),
             pltpu.SMEM((3, 2, NCLASS), jnp.float32),
             pltpu.SemaphoreType.DMA((3,)),
             pltpu.SemaphoreType.DMA((10,)),
@@ -417,9 +421,24 @@
             pltpu.SemaphoreType.DMA,
         ],
         compiler_params=pltpu.CompilerParams(
-            collective_id=0, has_side_effects=True, vmem_limit_bytes=64 * 2**20
+            collective_id=0, has_side_effects=True, vmem_limit_bytes=48 * 2**20
         ),
-    )(source, classes, table.transpose(2, 0, 1))
+    )(
+        pltpu.with_memory_space_constraint(source, pltpu.HBM),
+        pltpu.with_memory_space_constraint(classes, pltpu.HBM),
+        pltpu.with_memory_space_constraint(table.transpose(2, 0, 1), pltpu.HBM),
+    )
+    return pl.pallas_call(
+        finish,
+        out_shape=(
+            jax.ShapeDtypeStruct(source.shape, jnp.float32),
+            jax.ShapeDtypeStruct((ITERS,), jnp.float32),
+        ),
+        in_specs=[pl.BlockSpec(memory_space=pl.ANY), pl.BlockSpec(memory_space=pltpu.VMEM)],
+        out_specs=(pl.BlockSpec(memory_space=pltpu.HBM), pl.BlockSpec(memory_space=pltpu.SMEM)),
+        scratch_shapes=[pltpu.SemaphoreType.DMA],
+        compiler_params=pltpu.CompilerParams(vmem_limit_bytes=2**20),
+    )(held, totals)
 
 
 def solution(mesh):

time: 25.7 us -> 23 us (0.89)
  local copies, waits for them, and re-layouts: 2.08 us -> 0 us
  Pallas kernels: 22.8 us -> 22.2 us
    unnamed x4 -> x0, local copies, waits for them, and re-layouts: 2.08 us -> none
    pallas_call x1 -> x2, Pallas kernels: 22.8 us -> 22.2 us  [the longest x1 21 us: on_device(): pl.pallas_call(functools.partial(kernel, sizes), out_shape=(pltpu.VMEM(so...]
where the time goes in v3:
time: 23 us; the launch traced here: 22.8 us
  Pallas kernels  22.2 us (97%)
  between operations  0.64 us (3%)
    pallas_call x1, Pallas kernels, on_device(): pl.pallas_call(functools.partial(kernel, sizes), out_shape=(pltpu.VMEM(so...  21 us
    pallas_call x1, Pallas kernels, on_device(): pl.pallas_call(finish, out_shape=(jax.ShapeDtypeStruct(source.shape, jnp....  1.18 us

profile of v3, /device:TPU:0, one launch (start us, length us, event | category | flops | bytes accessed | tf_op | source)
XLA Modules:
  0.0 22.8 jit_solution(3509189338964637650)
XLA Ops:
  0.6 21.0 %shard_map.50 = (f32[1,4,64,128]{3,2,1,0:T(8,128)S(1)}, f32[1,128]{1,0:T(1,128)S(1)}) custom-call(f32[1,4,64,128]{3,2,1,0:T(8,128)} %source_hbm.1, s32[1,4,64,128]{3,2,1,0:T(8,128)} %classes_hbm.1, f32[3,2,8]{2,1,0:T(2,128)} %bitcast.1), custom_call_target="tpu_custom_call" | custom-call | tf_op jit(solution)/shard_map/pallas_call | solution.py:387
  21.6 1.2 %shard_map.51 = (f32[1,4,64,128]{3,2,1,0:T(8,128)}, f32[2]{0:T(128)}) custom-call(f32[1,4,64,128]{3,2,1,0:T(8,128)S(1)} %get-tuple-element.4.held, f32[1,128]{1,0:T(1,128)S(1)} %get-tuple-element.5.totals), custom_call_target="tpu_custom_call" | custom-call | tf_op jit(solution)/shard_map/pallas_call | solution.py:431

commit v4 on v3

--- a/solution.py
+++ b/solution.py
@@ -338,6 +338,14 @@
     tail(REACH)
     written = pltpu.make_async_copy(field.at[0, 0, pl.ds(1, layers), middle], out_hbm.at[0], out_sem)
     written.start()
+    for condition, copy in copies:
+
+        @pl.when(condition)
+        def _():
+            copy.wait_send()
+
+    across.wait_send()
+    written.wait()
     sent = []
     for number in range(len(groups)):
         for k, copy in enumerate(started):
@@ -348,20 +356,12 @@
             partial[number + 1] = total
             started = exchange(number + 1)
     totals[...] = total
-    for condition, copy in copies:
-
-        @pl.when(condition)
-        def _():
-            copy.wait_send()
-
     for copy in sent:
         copy.wait_send()
-    across.wait_send()
-    written.wait()
-
-
-def finish(held, totals, out_hbm, trace, sem):
-    copy = pltpu.make_async_copy(held, out_hbm, sem)
+
+
+def finish(held, totals, out_hbm, trace_hbm, trace, sem):
+    copy = pltpu.make_async_copy(held, out_hbm, sem.at[0])
     copy.start()
     total = totals[...]
     half = total.shape[1] // 2
@@ -370,6 +370,9 @@
         part = jnp.sum(jnp.where(lane // half == number, total, 0.0))
         root = jnp.sqrt(jnp.broadcast_to(part, total.shape))
         trace[number] = root[0, 0]
+    small = pltpu.make_async_copy(trace, trace_hbm, sem.at[1])
+    small.start()
+    small.wait()
     copy.wait()
 
 
@@ -435,8 +438,8 @@
             jax.ShapeDtypeStruct((ITERS,), jnp.float32),
         ),
         in_specs=[pl.BlockSpec(memory_space=pl.ANY), pl.BlockSpec(memory_space=pltpu.VMEM)],
-        out_specs=(pl.BlockSpec(memory_space=pltpu.HBM), pl.BlockSpec(memory_space=pltpu.SMEM)),
-        scratch_shapes=[pltpu.SemaphoreType.DMA],
+        out_specs=(pl.BlockSpec(memory_space=pltpu.HBM), pl.BlockSpec(memory_space=pltpu.HBM)),
+        scratch_shapes=[pltpu.SMEM((ITERS,), jnp.float32), pltpu.SemaphoreType.DMA((2,))],
         compiler_params=pltpu.CompilerParams(vmem_limit_bytes=2**20),
     )(held, totals)
 

time: 23 us -> 22.5 us (0.978)
  Pallas kernels: 22.2 us -> 21.7 us
    pallas_call x1, Pallas kernels: 1.18 us -> 0.74 us  [on_device(): pl.pallas_call(finish, out_shape=(jax.ShapeDtypeStruct(source.shape, jnp....]
where the time goes in v4:
time: 22.5 us; the launch traced here: 22.3 us
  Pallas kernels  21.7 us (96%)
  between operations  0.64 us (3%)
    pallas_call x1, Pallas kernels, on_device(): pl.pallas_call(functools.partial(kernel, sizes), out_shape=(pltpu.VMEM(so...  21 us
    pallas_call x1, Pallas kernels, on_device(): pl.pallas_call(finish, out_shape=(jax.ShapeDtypeStruct(source.shape, jnp....  0.74 us

profile of v4, /device:TPU:0, one launch (start us, length us, event | category | flops | bytes accessed | tf_op | source)
XLA Modules:
  0.0 22.3 jit_solution(10177816369651076011)
XLA Ops:
  0.6 21.0 %shard_map.50 = (f32[1,4,64,128]{3,2,1,0:T(8,128)S(1)}, f32[1,128]{1,0:T(1,128)S(1)}) custom-call(f32[1,4,64,128]{3,2,1,0:T(8,128)} %source_hbm.1, s32[1,4,64,128]{3,2,1,0:T(8,128)} %classes_hbm.1, f32[3,2,8]{2,1,0:T(2,128)} %bitcast.1), custom_call_target="tpu_custom_call" | custom-call | tf_op jit(solution)/shard_map/pallas_call | solution.py:390
  21.6 0.7 %shard_map.51 = (f32[1,4,64,128]{3,2,1,0:T(8,128)}, f32[2]{0:T(128)}) custom-call(f32[1,4,64,128]{3,2,1,0:T(8,128)S(1)} %get-tuple-element.4.held, f32[1,128]{1,0:T(1,128)S(1)} %get-tuple-element.5.totals), custom_call_target="tpu_custom_call" | custom-call | tf_op jit(solution)/shard_map/pallas_call | solution.py:434
